TPU v7x, 256 devices: a whole 4x4x8 slice. The times are simulated.
256 devices in a mesh: ctx: 32 (over z_hi, x, y), fsdp: 8 (over z_lo, core).
Axes of the slice: x: 4, y: 4, z: 8 (z_hi: 2, z_lo: 4; z = z_hi * 4 + z_lo), core: 2. Of those that a mesh axis runs over, the one named last changes fastest.
Arguments:
- out_grad: bfloat16 [4096, 32768], P('fsdp', 'ctx'), may hold values from -6 to 6
- gate_values: bfloat16 [4096, 32768], P('fsdp', 'ctx'), may hold values from -6 to 6
- kv_product: bfloat16 [4096, 32768], P('fsdp', 'ctx'), may hold values from -6 to 6
- w_out: bfloat16 [4096, 4096], P('ctx', 'fsdp'), may hold values from -0.09375 to 0.09375
- filters: bfloat16 [8, 32, 16, 128], P('fsdp', 'ctx'), may hold values from -0.5 to 0.5
Outputs:
- gate_grad: float32 [4096, 32768], P('fsdp', 'ctx')
- kv_grad: bfloat16 [4096, 32768], P('fsdp', 'ctx')
- filter_grad: float32 [8, 32, 16, 128], P('fsdp', 'ctx')
- w_grad: float32 [4096, 4096], P('ctx', 'fsdp')
All inputs are finite; a program needn't handle non-finite values.
Results may differ from a plain program's by a relative error of at most 0.0049.
Values may be sent and summed in bfloat16 or wider, within the bound.
A program may use at most 128 MiB of HBM per device.

v0:
```python
import math
import jax
import jax.numpy as jnp
from jax import lax
from jax.sharding import PartitionSpec as P


def toeplitz_pair(filters):
    channels, tap_count = filters.shape
    zero_pad = jnp.zeros_like(filters)

    def make_band(vector):
        tiled = jnp.tile(vector, (1, tap_count + 1))
        window_cut = tiled[:, tap_count : tap_count + tap_count * (2 * tap_count - 1)]
        return window_cut.reshape(channels, tap_count, 2 * tap_count - 1)[:, :, :tap_count]

    near_band = make_band(jnp.concatenate([zero_pad, filters], axis=1))
    far_band = make_band(jnp.concatenate([filters, zero_pad], axis=1))
    return (near_band, far_band)


def mixer_piece(filters, signal, signal_prior, cotangent, cotangent_after):
    channels, seq_len = signal.shape
    tap_count = filters.shape[1]
    blocks_count = seq_len // tap_count
    near_band, far_band = toeplitz_pair(filters)
    current = signal.reshape(channels, blocks_count, tap_count)
    previous = jnp.concatenate([signal_prior[:, None, :], current[:, :-1]], axis=1)
    grad_current = cotangent.reshape(channels, blocks_count, tap_count)
    grad_later = jnp.concatenate([grad_current[:, 1:], cotangent_after[:, None, :]], axis=1)
    wide = jnp.float32
    mixed = jnp.einsum("cbs,csr->cbr", current, near_band, preferred_element_type=wide)
    mixed = mixed + jnp.einsum("cbs,csr->cbr", previous, far_band, preferred_element_type=wide)
    signal_grad = jnp.einsum("cbr,csr->cbs", grad_current, near_band, preferred_element_type=wide)
    signal_grad = signal_grad + jnp.einsum(
        "cbr,csr->cbs", grad_later, far_band, preferred_element_type=wide
    )
    near_weight = jnp.einsum("cbs,cbr->csr", current, grad_current, preferred_element_type=wide)
    far_weight = jnp.einsum("cbs,cbr->csr", previous, grad_current, preferred_element_type=wide)
    band_pair, pullback = jax.vjp(toeplitz_pair, filters.astype(jnp.float32))
    filter_part = pullback((near_weight, far_weight))[0]
    return (mixed.reshape(channels, seq_len), signal_grad.reshape(channels, seq_len), filter_part)


def on_device(out_grad, gate_values, kv_product, w_out, filters):
    ctx_count = lax.axis_size("ctx")
    chan_count = filters.shape[2]
    tap_count = filters.shape[3]
    norm_scale = 1.0 / math.sqrt(ctx_count * out_grad.shape[1])
    grad_full = lax.all_gather(out_grad, "fsdp", axis=0, tiled=True)
    grad_part = grad_full
    mix_grad = lax.dot_general(
        lax.all_gather(w_out, "ctx", axis=0, tiled=True),
        grad_part,
        (((0,), (0,)), ((), ())),
        preferred_element_type=jnp.float32,
    )
    conv_grad = (mix_grad * gate_values.astype(jnp.float32)).astype(jnp.bfloat16)
    signal_chan, grad_chan = (
        lax.all_to_all(kv_product, "ctx", split_axis=0, concat_axis=1, tiled=True),
        lax.all_to_all(conv_grad, "ctx", split_axis=0, concat_axis=1, tiled=True),
    )
    own_filters = filters.reshape(chan_count, tap_count)
    edge_zero = jnp.zeros((chan_count, tap_count), jnp.bfloat16)
    mixed, signal_grad, filter_part = mixer_piece(
        own_filters, signal_chan, edge_zero, grad_chan, edge_zero
    )
    mixed_tok, kv_grad = (
        lax.all_to_all(mixed.astype(jnp.bfloat16), "ctx", split_axis=1, concat_axis=0, tiled=True),
        lax.all_to_all(
            signal_grad.astype(jnp.bfloat16), "ctx", split_axis=1, concat_axis=0, tiled=True
        ),
    )
    filter_grad = (filter_part * norm_scale).reshape(filters.shape)
    mixed_wide = mixed_tok.astype(jnp.float32)
    gate_grad = mix_grad * mixed_wide
    gated_rows = (gate_values.astype(jnp.float32) * mixed_wide).astype(jnp.bfloat16)
    grad_part = grad_full
    w_grad = (
        lax.psum_scatter(
            lax.dot_general(
                grad_part, gated_rows, (((1,), (1,)), ((), ())), preferred_element_type=jnp.float32
            ),
            "ctx",
            scatter_dimension=0,
            tiled=True,
        )
        * norm_scale
    )
    return (gate_grad, kv_grad, filter_grad, w_grad)


def solution(mesh):
    in_specs = (
        P("fsdp", "ctx"),
        P("fsdp", "ctx"),
        P("fsdp", "ctx"),
        P("ctx", "fsdp"),
        P("fsdp", "ctx", None, None),
    )
    out_specs = (P("fsdp", "ctx"), P("fsdp", "ctx"), P("fsdp", "ctx", None, None), P("ctx", "fsdp"))
    return jax.shard_map(
        on_device, mesh=mesh, in_specs=in_specs, out_specs=out_specs, check_vma=False
    )
```

profile of v0, /device:TPU:32, one launch (start us, length us, event | category | flops | bytes accessed | tf_op | source)
XLA Modules:
  0.0 575.9 jit_solution(2997700983290757412)
XLA Ops:
  7.2 0.7 all-gather.3.cloned.1.call-update
  8.0 0.7 all-gather.5.cloned.1.call-update
  8.7 13.1 %all-to-all-start = ((bf16[32,16,1024]{2,1,0:T(8,128)(2,1)}), bf16[32,16,1024]{2,1,0:T(8,128)(2,1)S(1)}, u32[]{:S(2)}, u32[]{:S(2)}) async-start(bf16[32,16,1024]{2,1,0:T(8,128)(2,1)} %bitcast.45), calls=%async_computation | async-start | bytes 2097152 | tf_op jit(solution)/shard_map/all_to_all | solution.py:60
  22.2 3.4 reshape.73
  25.6 0.2 copy.47
  25.8 1.0 slice.24
  26.9 4.6 reshape.71
  31.5 23.4 %all-to-all-done = bf16[32,16,1024]{2,1,0:T(8,128)(2,1)S(1)} async-done(((bf16[32,16,1024]{2,1,0:T(8,128)(2,1)}), bf16[32,16,1024]{2,1,0:T(8,128)(2,1)S(1)}, u32[]{:S(2)}, u32[]{:S(2)}) %all-to-all-start) | async-done | bytes 1048608 | tf_op jit(solution)/shard_map/all_to_all | solution.py:60
  55.0 1.5 copy.30
  56.5 1.5 reshape.72
  58.0 0.5 fusion.6
  58.6 1.5 fusion.2
  60.0 1.6 copy.32
  61.7 1.3 convert_element_type.34
  62.9 1.8 copy.33
  64.7 31.7 %all_to_all.58 = bf16[16,32,1024]{2,0,1:T(8,128)(2,1)} all-to-all(bf16[16,32,1024]{2,0,1:T(8,128)(2,1)S(1)} %copy.33), channel_id=1, replica_groups=mesh['ctx'=32,'fsdp'=8] {'ctx'}, dimensions={1} | all-to-all | bytes 2097152 | tf_op jit(solution)/shard_map/all_to_all | solution.py:69
  96.5 51.4 %all-gather.3.cloned.1.call-done = bf16[4096,512]{1,0:T(8,128)(2,1)} async-done(((bf16[128,512]{1,0:T(8,128)(2,1)}), bf16[4096,512]{1,0:T(8,128)(2,1)}) %all-gather.3.cloned.1.call-update) | async-done | bytes 4194320 | tf_op jit(solution)/shard_map/all_gather | solution.py:53
  147.9 86.7 %all-gather.5.cloned.1.call-done = bf16[4096,1024]{1,0:T(8,128)(2,1)} async-done(((bf16[512,1024]{1,0:T(8,128)(2,1)}), bf16[4096,1024]{1,0:T(8,128)(2,1)}) %all-gather.5.cloned.1.call-update) | async-done | bytes 8388624 | tf_op jit(solution)/shard_map/all_gather | solution.py:50
  234.6 11.6 %fusion = (bf16[512,1024]{1,0:T(8,128)(2,1)}, f32[512,1024]{1,0:T(8,128)}, bf16[512,1024]{1,0:T(8,128)(2,1)S(1)}) fusion(bf16[512,1024]{1,0:T(8,128)(2,1)} %param.6, bf16[16,32,1024]{2,0,1:T(8,128)(2,1)} %all_to_all.58, bf16[4096,512]{1,0:T(8,128)(2,1)} %all-gather.3.cloned.1.call-done, bf16[4096,1024]{1,0:T(8,128)(2,1)} %all-gather.5.cloned.1.call-done), kind=kOutput, calls=%fused_computation.3 | convolution fusion | flops 4298637312 | bytes 18874368 | tf_op jit(solution)/shard_map/dot_general | solution.py:52
  246.2 6.9 %convolution_bitcast_fusion = f32[4096,512]{0,1:T(8,128)} fusion(bf16[512,1024]{1,0:T(8,128)(2,1)S(1)} %get-tuple-element.18, bf16[4096,1024]{1,0:T(8,128)(2,1)S(1)} %copy-done.3), kind=kOutput, calls=%fused_computation | convolution fusion | flops 4294967296 | bytes 17825792 | tf_op jit(solution)/shard_map/dot_general | solution.py:81
  253.1 59.1 %all_to_all.59 = bf16[32,16,1024]{2,1,0:T(8,128)(2,1)S(1)} all-to-all(bf16[32,16,1024]{2,1,0:T(8,128)(2,1)} %bitcast.46), channel_id=1, replica_groups=mesh['ctx'=32,'fsdp'=8] {'ctx'}, dimensions={0} | all-to-all | bytes 2097152 | tf_op jit(solution)/shard_map/all_to_all | solution.py:61
  312.2 1.5 copy.34
  313.7 1.5 reshape.74
  315.3 0.3 slice.29
  315.6 0.9 copy-done.1
  316.5 0.4 fusion.11
  316.9 1.4 add_convert_fusion
  318.4 1.5 convert_element_type.41
  319.9 1.5 copy.36
  321.4 5.2 all-to-all-start.3
  326.7 0.5 convolution_bitcast_fusion.1
  327.2 1.3 copy.46
  328.5 2.8 pad.18.clone
  331.3 4.2 reshape.77
  335.4 3.0 pad.19
  338.5 2.9 reshape.78
  341.3 1.8 reduce_sum.19
  343.1 0.6 fusion.4
  343.7 0.2 pad.16
  343.9 2.6 reshape.75
  346.5 3.1 pad.17
  349.5 1.7 reshape.76
  351.5 0.6 fusion.14
  352.1 3.0 all-to-all-done.3
  355.0 210.2 %reduce-scatter.2.cloned.1.call-done = f32[128,512]{0,1:T(8,128)} async-done(((f32[4096,512]{0,1:T(8,128)}), f32[128,512]{0,1:T(8,128)}) %reduce-scatter.2.cloned.1.call-update) | async-done | bytes 262160 | tf_op jit(solution)/shard_map/reduce_scatter | solution.py:80
  565.3 1.0 broadcast_multiply_fusion
  566.3 0.8 copy.40
  567.1 2.3 copy.50
  (17 shorter events, 0.8 us)
Async XLA Ops:
  7.2 14.6 %copy-start.2 = (bf16[1,1,16,128]{3,2,1,0:T(8,128)(2,1)S(1)}, bf16[1,1,16,128]{3,2,1,0:T(8,128)(2,1)}, u32[]{:S(2)}) copy-start(bf16[1,1,16,128]{3,2,1,0:T(8,128)(2,1)} %param.9) | copy-start | bytes 12292
  7.2 140.7 %all-gather.3.cloned.1.call-start = ((), (), s32[]{:S(2)}) async-start(), calls=%async_computation.5 | async-start | bytes 4325376 | tf_op jit(solution)/shard_map/all_gather | solution.py:53
  7.9 226.7 %all-gather.5.cloned.1.call-start = ((), (), s32[]{:S(2)}) async-start(), calls=%async_computation.6 | async-start | bytes 9437184 | tf_op jit(solution)/shard_map/all_gather | solution.py:50
  8.7 46.3 %all-to-all-start = ((bf16[32,16,1024]{2,1,0:T(8,128)(2,1)}), bf16[32,16,1024]{2,1,0:T(8,128)(2,1)S(1)}, u32[]{:S(2)}, u32[]{:S(2)}) async-start(bf16[32,16,1024]{2,1,0:T(8,128)(2,1)} %bitcast.45), calls=%async_computation | async-start | bytes 2097152 | tf_op jit(solution)/shard_map/all_to_all | solution.py:60
  21.7 543.6 %reduce-scatter.2.cloned.1.call-start = ((), (), s32[]{:S(2)}) async-start(), calls=%async_computation.7 | async-start | bytes 8650752 | tf_op jit(solution)/shard_map/reduce_scatter | solution.py:80
  31.5 27.0 %copy-start = (bf16[16,128,255]{2,1,0:T(8,128)(2,1)}, bf16[16,128,255]{2,1,0:T(8,128)(2,1)S(1)}, u32[]{:S(2)}) copy-start(bf16[16,128,255]{2,1,0:T(8,128)(2,1)S(1)} %reshape.71) | copy-start | bytes 3133444
  234.6 11.6 %copy-start.3 = (bf16[4096,1024]{1,0:T(8,128)(2,1)S(1)}, bf16[4096,1024]{1,0:T(8,128)(2,1)}, u32[]{:S(2)}) copy-start(bf16[4096,1024]{1,0:T(8,128)(2,1)} %all-gather.5.cloned.1.call-done) | copy-start | bytes 25165828
  315.3 1.2 copy-start.1
  321.4 33.6 %all-to-all-start.3 = ((bf16[16,32,1024]{2,0,1:T(8,128)(2,1)}), bf16[16,32,1024]{2,0,1:T(8,128)(2,1)}, u32[]{:S(2)}, u32[]{:S(2)}) async-start(bf16[16,32,1024]{2,0,1:T(8,128)(2,1)} %copy.36), calls=%async_computation.3 | async-start | bytes 2097152 | tf_op jit(solution)/shard_map/all_to_all | solution.py:70
Sparse Core Ops, SparseCore 0:
  11.5 136.3 all-gather.2
  149.7 84.8 all-gather.4
  253.2 312.0 reduce-scatter.1
where the time goes:
time: 577 us; the launch traced here: 576 us
  waiting for transfers between devices  376 us (65%)
  blocking collectives  90.8 us (16%)
  local copies, waits for them, and re-layouts  49.6 us (9%)
  matrix products  23.3 us (4%)
  starting transfers between devices  18.4 us (3%)
  between operations  14 us (2%)
    reduce_scatter x1, waiting for transfers between devices, on_device(): lax.psum_scatter(lax.dot_general(grad_part, gated_rows, (((1,), (1,)), ((...  210 us
    all_gather x1, waiting for transfers between devices, on_device(): grad_full = lax.all_gather(out_grad, 'fsdp', axis=0, tiled=True)  86.7 us
    all_to_all x1, blocking collectives, on_device(): lax.all_to_all(conv_grad, 'ctx', split_axis=0, concat_axis=1, tiled=True)  59.1 us
    all_gather x1, waiting for transfers between devices, on_device(): lax.all_gather(w_out, 'ctx', axis=0, tiled=True)  51.4 us
    all_to_all x1, blocking collectives, on_device(): lax.all_to_all(mixed.astype(jnp.bfloat16), 'ctx', split_axis=1, concat_ax...  31.7 us
    all_to_all x1, waiting for transfers between devices, on_device(): lax.all_to_all(kv_product, 'ctx', split_axis=0, concat_axis=1, tiled=True)  23.4 us
    reshape x4, local copies, waits for them, and re-layouts, make_band(): window_cut.reshape(channels, tap_count, 2 * tap_count - 1)[:, :, :tap_count]  14.7 us
    all_to_all x1, starting transfers between devices, on_device(): lax.all_to_all(kv_product, 'ctx', split_axis=0, concat_axis=1, tiled=True)  13.1 us
  transfers between devices with their start and end apart: 5, of which 5 were waited for; matrix products, arithmetic and copies ran while one was open for 9% of the time, Pallas kernels for 0%

commit v1 on v0

--- a/solution.py
+++ b/solution.py
@@ -3,6 +3,12 @@
 import jax.numpy as jnp
 from jax import lax
 from jax.sharding import PartitionSpec as P
+
+
+def _extend_roots(state, mesh_ax):
+    return jnp.concatenate(
+        lax.all_to_all(jnp.stack(jnp.split(state, lax.axis_size(mesh_ax), 1), 0), mesh_ax, 0, 0), 0
+    )
 
 
 def toeplitz_pair(filters):
@@ -66,7 +72,7 @@
         own_filters, signal_chan, edge_zero, grad_chan, edge_zero
     )
     mixed_tok, kv_grad = (
-        lax.all_to_all(mixed.astype(jnp.bfloat16), "ctx", split_axis=1, concat_axis=0, tiled=True),
+        _extend_roots(mixed.astype(jnp.bfloat16), "ctx"),
         lax.all_to_all(
             signal_grad.astype(jnp.bfloat16), "ctx", split_axis=1, concat_axis=0, tiled=True
         ),

time: 577 us -> 558 us (0.967)
  waiting for transfers between devices: 376 us -> 341 us
  blocking collectives: 90.8 us -> 99 us
    all_gather x1, waiting for transfers between devices: 86.7 us -> 30.9 us  [on_device(): grad_full = lax.all_gather(out_grad, 'fsdp', axis=0, tiled=True)]
    all_gather x1, waiting for transfers between devices: 51.4 us -> 105 us  [on_device(): lax.all_gather(w_out, 'ctx', axis=0, tiled=True)]
    reduce_scatter x1, waiting for transfers between devices: 210 us -> 158 us  [on_device(): lax.psum_scatter(lax.dot_general(grad_part, gated_rows, (((1,), (1,)), ((...]
    all_to_all x1, blocking collectives: 31.7 us -> 44.9 us  [_extend_roots(): lax.all_to_all(jnp.stack(jnp.split(state, lax.axis_size(mesh_ax), 1), 0),...]
    all_to_all x1, waiting for transfers between devices: 2.97 us -> 15 us  [on_device(): lax.all_to_all(signal_grad.astype(jnp.bfloat16), 'ctx', split_axis=1, con...]
    all_to_all x1, waiting for transfers between devices: 23.4 us -> 31.2 us  [on_device(): lax.all_to_all(kv_product, 'ctx', split_axis=0, concat_axis=1, tiled=True)]
  transfers between devices with their start and end apart: 5 -> 5, of which waited for: 5 -> 5; matrix products, arithmetic and copies ran while one was open for 9% -> 13% of each run, Pallas kernels for 0% -> 0%
where the time goes in v1:
time: 558 us; the launch traced here: 552 us
  waiting for transfers between devices  341 us (61%)
  blocking collectives  99 us (18%)
  local copies, waits for them, and re-layouts  47.2 us (8%)
  matrix products  27.1 us (5%)
  starting transfers between devices  20.1 us (4%)
  between operations  14.2 us (3%)
    reduce_scatter x1, waiting for transfers between devices, on_device(): lax.psum_scatter(lax.dot_general(grad_part, gated_rows, (((1,), (1,)), ((...  158 us
    all_gather x1, waiting for transfers between devices, on_device(): lax.all_gather(w_out, 'ctx', axis=0, tiled=True)  105 us
    all_to_all x1, blocking collectives, on_device(): lax.all_to_all(conv_grad, 'ctx', split_axis=0, concat_axis=1, tiled=True)  54.2 us
    all_to_all x1, blocking collectives, _extend_roots(): lax.all_to_all(jnp.stack(jnp.split(state, lax.axis_size(mesh_ax), 1), 0),...  44.9 us
    all_to_all x1, waiting for transfers between devices, on_device(): lax.all_to_all(kv_product, 'ctx', split_axis=0, concat_axis=1, tiled=True)  31.2 us
    all_gather x1, waiting for transfers between devices, on_device(): grad_full = lax.all_gather(out_grad, 'fsdp', axis=0, tiled=True)  30.9 us
    all_to_all x1, waiting for transfers between devices, on_device(): lax.all_to_all(signal_grad.astype(jnp.bfloat16), 'ctx', split_axis=1, con...  15 us
    reshape x4, local copies, waits for them, and re-layouts, make_band(): window_cut.reshape(channels, tap_count, 2 * tap_count - 1)[:, :, :tap_count]  14.5 us
  transfers between devices with their start and end apart: 5, of which 5 were waited for; matrix products, arithmetic and copies ran while one was open for 13% of the time, Pallas kernels for 0%

profile of v1, /device:TPU:32, one launch (start us, length us, event | category | flops | bytes accessed | tf_op | source)
XLA Modules:
  0.0 552.3 jit_solution(14414515279667108531)
XLA Ops:
  7.2 0.7 all-gather.5.cloned.1.call-update
  7.9 13.1 %all-to-all-start = ((bf16[32,16,1024]{2,1,0:T(8,128)(2,1)}), bf16[32,16,1024]{2,1,0:T(8,128)(2,1)S(1)}, u32[]{:S(2)}, u32[]{:S(2)}) async-start(bf16[32,16,1024]{2,1,0:T(8,128)(2,1)} %bitcast.207), calls=%async_computation | async-start | bytes 2097152 | tf_op jit(solution)/shard_map/all_to_all | solution.py:66
  21.0 0.7 all-gather.3.cloned.1.call-update
  21.9 0.2 copy.46
  22.2 3.4 reshape.70
  25.6 0.2 copy.45
  25.8 1.0 slice.24
  26.9 4.6 reshape.68
  31.5 31.2 %all-to-all-done = bf16[32,16,1024]{2,1,0:T(8,128)(2,1)S(1)} async-done(((bf16[32,16,1024]{2,1,0:T(8,128)(2,1)}), bf16[32,16,1024]{2,1,0:T(8,128)(2,1)S(1)}, u32[]{:S(2)}, u32[]{:S(2)}) %all-to-all-start) | async-done | bytes 1048608 | tf_op jit(solution)/shard_map/all_to_all | solution.py:66
  62.7 1.5 copy.29
  64.2 1.5 reshape.69
  65.8 0.5 fusion.7
  66.3 1.5 fusion.2
  67.8 1.6 copy.31
  69.4 0.7 copy.49
  70.5 44.9 %all_to_all.53 = bf16[32,16,1024]{2,1,0:T(8,128)(2,1)S(1)} all-to-all(bf16[32,16,1024]{2,1,0:T(8,128)(2,1)S(1)} %constant_dynamic-update-slice_fusion), channel_id=1, replica_groups=mesh['ctx'=32,'fsdp'=8] {'ctx'}, dimensions={0} | all-to-all | bytes 2097152 | tf_op jit(solution)/shard_map/all_to_all | solution.py:10
  115.4 30.9 %all-gather.5.cloned.1.call-done = bf16[4096,1024]{1,0:T(8,128)(2,1)} async-done(((bf16[512,1024]{1,0:T(8,128)(2,1)}), bf16[4096,1024]{1,0:T(8,128)(2,1)}) %all-gather.5.cloned.1.call-update) | async-done | bytes 8388624 | tf_op jit(solution)/shard_map/all_gather | solution.py:56
  146.3 11.5 %convolution_bitcast_fusion = f32[4096,512]{0,1:T(8,128)} fusion(bf16[4096,1024]{1,0:T(8,128)(2,1)} %all-gather.5.cloned.1.call-done, bf16[512,1024]{1,0:T(8,128)(2,1)S(1)} %bitcast.208, bf16[512,1024]{1,0:T(8,128)(2,1)} %param.6), kind=kOutput, calls=%fused_computation | convolution fusion | flops 4297064448 | bytes 18874368 | tf_op jit(solution)/shard_map/dot_general | solution.py:87
  157.8 104.9 %all-gather.3.cloned.1.call-done = bf16[4096,512]{1,0:T(8,128)(2,1)} async-done(((bf16[128,512]{1,0:T(8,128)(2,1)}), bf16[4096,512]{1,0:T(8,128)(2,1)}) %all-gather.3.cloned.1.call-update) | async-done | bytes 4194320 | tf_op jit(solution)/shard_map/all_gather | solution.py:59
  262.6 10.7 %fusion = (bf16[512,1024]{1,0:T(8,128)(2,1)S(1)}, f32[512,1024]{1,0:T(8,128)}) fusion(bf16[512,1024]{1,0:T(8,128)(2,1)} %param.6, bf16[32,16,1024]{2,1,0:T(8,128)(2,1)S(1)} %all_to_all.53, bf16[4096,512]{1,0:T(8,128)(2,1)} %all-gather.3.cloned.1.call-done, bf16[4096,1024]{1,0:T(8,128)(2,1)} %all-gather.5.cloned.1.call-done), kind=kOutput, calls=%fused_computation.4 | convolution fusion | flops 4297588736 | bytes 17825792 | tf_op jit(solution)/shard_map/dot_general | solution.py:58
  273.3 54.2 %all_to_all.54 = bf16[32,16,1024]{2,1,0:T(8,128)(2,1)S(1)} all-to-all(bf16[32,16,1024]{2,1,0:T(8,128)(2,1)S(1)} %bitcast.209), channel_id=1, replica_groups=mesh['ctx'=32,'fsdp'=8] {'ctx'}, dimensions={0} | all-to-all | bytes 2097152 | tf_op jit(solution)/shard_map/all_to_all | solution.py:67
  327.5 1.5 copy.32
  329.1 1.5 reshape.71
  330.6 0.3 slice.29
  330.9 0.9 copy-done.1
  331.8 0.4 fusion.12
  332.2 1.4 add_convert_fusion
  333.7 1.5 convert_element_type.36
  335.2 1.5 copy.34
  336.7 6.9 %all-to-all-start.3 = ((bf16[16,32,1024]{2,0,1:T(8,128)(2,1)}), bf16[16,32,1024]{2,0,1:T(8,128)(2,1)}, u32[]{:S(2)}, u32[]{:S(2)}) async-start(bf16[16,32,1024]{2,0,1:T(8,128)(2,1)} %copy.34), calls=%async_computation.3 | async-start | bytes 2097152 | tf_op jit(solution)/shard_map/all_to_all | solution.py:76
  343.7 0.5 convolution_bitcast_fusion.1
  344.2 1.3 copy.44
  345.5 2.8 pad.18.clone
  348.3 4.1 reshape.74
  352.4 3.1 pad.19
  355.4 2.8 reshape.75
  358.2 1.8 reduce_sum.19
  360.0 0.6 fusion.5
  360.6 0.2 pad.16
  360.8 2.5 reshape.72
  363.3 3.1 pad.17
  366.4 1.7 reshape.73
  368.3 0.6 fusion.15
  368.9 15.0 %all-to-all-done.3 = bf16[16,32,1024]{2,0,1:T(8,128)(2,1)} async-done(((bf16[16,32,1024]{2,0,1:T(8,128)(2,1)}), bf16[16,32,1024]{2,0,1:T(8,128)(2,1)}, u32[]{:S(2)}, u32[]{:S(2)}) %all-to-all-start.3) | async-done | bytes 1048608 | tf_op jit(solution)/shard_map/all_to_all | solution.py:76
  383.9 157.8 %reduce-scatter.2.cloned.1.call-done = f32[128,512]{0,1:T(8,128)} async-done(((f32[4096,512]{0,1:T(8,128)}), f32[128,512]{0,1:T(8,128)}) %reduce-scatter.2.cloned.1.call-update) | async-done | bytes 262160 | tf_op jit(solution)/shard_map/reduce_scatter | solution.py:86
  541.7 1.0 broadcast_multiply_fusion
  542.7 0.8 copy.38
  543.5 2.3 copy.82
  (46 shorter events, 0.7 us)
Async XLA Ops:
  7.2 14.6 %copy-start.2 = (bf16[1,1,16,128]{3,2,1,0:T(8,128)(2,1)S(1)}, bf16[1,1,16,128]{3,2,1,0:T(8,128)(2,1)}, u32[]{:S(2)}) copy-start(bf16[1,1,16,128]{3,2,1,0:T(8,128)(2,1)} %param.9) | copy-start | bytes 12292
  7.2 139.1 %all-gather.5.cloned.1.call-start = ((), (), s32[]{:S(2)}) async-start(), calls=%async_computation.6 | async-start | bytes 9437184 | tf_op jit(solution)/shard_map/all_gather | solution.py:56
  7.9 54.8 %all-to-all-start = ((bf16[32,16,1024]{2,1,0:T(8,128)(2,1)}), bf16[32,16,1024]{2,1,0:T(8,128)(2,1)S(1)}, u32[]{:S(2)}, u32[]{:S(2)}) async-start(bf16[32,16,1024]{2,1,0:T(8,128)(2,1)} %bitcast.207), calls=%async_computation | async-start | bytes 2097152 | tf_op jit(solution)/shard_map/all_to_all | solution.py:66
  21.0 241.7 %all-gather.3.cloned.1.call-start = ((), (), s32[]{:S(2)}) async-start(), calls=%async_computation.5 | async-start | bytes 4325376 | tf_op jit(solution)/shard_map/all_gather | solution.py:59
  21.7 520.0 %reduce-scatter.2.cloned.1.call-start = ((), (), s32[]{:S(2)}) async-start(), calls=%async_computation.7 | async-start | bytes 8650752 | tf_op jit(solution)/shard_map/reduce_scatter | solution.py:86
  31.5 34.8 %copy-start = (bf16[16,128,255]{2,1,0:T(8,128)(2,1)}, bf16[16,128,255]{2,1,0:T(8,128)(2,1)S(1)}, u32[]{:S(2)}) copy-start(bf16[16,128,255]{2,1,0:T(8,128)(2,1)S(1)} %reshape.68) | copy-start | bytes 3133444
  330.6 1.2 copy-start.1
  336.7 47.1 %all-to-all-start.3 = ((bf16[16,32,1024]{2,0,1:T(8,128)(2,1)}), bf16[16,32,1024]{2,0,1:T(8,128)(2,1)}, u32[]{:S(2)}, u32[]{:S(2)}) async-start(bf16[16,32,1024]{2,0,1:T(8,128)(2,1)} %copy.34), calls=%async_computation.3 | async-start | bytes 2097152 | tf_op jit(solution)/shard_map/all_to_all | solution.py:76
Sparse Core Ops, SparseCore 0:
  9.8 136.4 all-gather.4
  149.8 112.8 all-gather.2
  265.2 276.4 reduce-scatter.1
